TPU v7x, 128 devices: a whole 4x4x4 slice. The times are simulated.
128 devices in a mesh: curve: 128 (over y, x, z, core).
Axes of the slice: x: 4, y: 4, z: 4, core: 2. Of those that a mesh axis runs over, the one named last changes fastest.
Arguments:
- diag_blocks: bfloat16 [8192, 128, 128], P('curve'), may hold values from 0.049804688 to 1
- super_blocks: bfloat16 [8192, 4, 128, 128], P('curve'), may hold values from 0.049804688 to 1
- far_blocks: bfloat16 [32768, 128, 128], P('curve'), may hold values from 0.049804688 to 1
- far_row: int32 [32768], P('curve'), may hold values from -1 to 63, as said below
- send_slot: int32 [32768], P('curve'), may hold values from -1 to 63, as said below
- start_panel: float32 [64, 1048576], P(None, 'curve'), may hold values from -6 to 6
Outputs:
- basis: float32 [64, 1048576], P(None, 'curve')
- update: float32 [64, 1048576], P(None, 'curve')
Inputs may be any that keep to these rules, and one draw needn't show every extreme that they name: `send_slot`: at most 2 live slots from one owner to one reader; some owner fills all 2 slots to every reader. `far_row`: empty slots match those of send_slot.
All inputs are finite; a program needn't handle non-finite values.
Results may differ from a plain program's by a relative error of at most 0.0026.
Values may be sent and summed in bfloat16 or wider, within the bound.
A program may use at most 256 MiB of HBM per device.

v0:
```python
import jax
import jax.numpy as jnp
from jax import lax
from jax.sharding import PartitionSpec as P

ITERS = 2
exact_mode = lax.Precision.HIGHEST
step_size = 10.0
momentum = 0.5


def extended_2(array, sides, width):
    for axis, dim in sides:
        size, length = (lax.axis_size(axis), array.shape[dim])
        up = [(i, (i + 1) % size) for i in range(size)]
        down = [(j, i) for i, j in up]
        last = lax.slice_in_dim(array, length - width, length, axis=dim)
        initial = lax.slice_in_dim(array, 0, width, axis=dim)
        before = lax.ppermute(last, axis, up)
        after = lax.ppermute(initial, axis, down)
        array = jnp.concatenate([before, array, after], axis=dim)
    return array


def passed_along(block, axis, distance):
    devices = range(lax.axis_size(axis))
    route = [((i - distance) % len(devices), i) for i in devices]
    return lax.ppermute(block, axis, route)


def gram_of(first, second):
    return jnp.einsum("bip,bjp->ij", first, second, precision=exact_mode)


def lower_inverse(cross):
    factor = jnp.linalg.cholesky(cross)
    return lax.linalg.triangular_solve(
        factor, jnp.eye(cross.shape[0], dtype=cross.dtype), left_side=True, lower=True
    )


def left_apply(matrix, blocks):
    return jnp.einsum("ij,bjp->bip", matrix, blocks, precision=exact_mode)


def near_apply(panel, diag_blocks, super_blocks, edge_supers):
    bands = super_blocks.shape[1]
    rows_dev = panel.shape[0]
    extended = extended_2(panel, (("curve", 0),), bands)
    supers_ext = jnp.concatenate([edge_supers, super_blocks], axis=0)
    result = jnp.einsum("bcp,bqp->bcq", panel, diag_blocks, preferred_element_type=jnp.float32)
    result = result + jnp.einsum(
        "bcp,bpq->bcq", panel, diag_blocks, preferred_element_type=jnp.float32
    )
    for band in range(bands):
        ahead = extended[bands + band + 1 : bands + band + 1 + rows_dev]
        result = result + jnp.einsum(
            "bcp,bqp->bcq", ahead, super_blocks[:, band], preferred_element_type=jnp.float32
        )
        first = bands - band - 1
        behind = extended[first : first + rows_dev]
        result = result + jnp.einsum(
            "bcp,bpq->bcq",
            behind,
            supers_ext[first : first + rows_dev, band],
            preferred_element_type=jnp.float32,
        )
    return result


def shards(diag_blocks, super_blocks, far_blocks, far_row, send_slot, start_panel):
    bands = super_blocks.shape[1]
    rows_dev = diag_blocks.shape[0]
    block_size = diag_blocks.shape[1]
    width = start_panel.shape[0]
    total_points = rows_dev * block_size * lax.axis_size("curve")
    edge_supers = passed_along(super_blocks[rows_dev - bands :], "curve", 1)
    send_live = (send_slot >= 0)[:, None, None]
    send_index = jnp.maximum(send_slot, 0)
    recv_live = (far_row >= 0)[:, None, None]
    recv_index = jnp.maximum(far_row, 0)

    def apply_w(panel):
        result = near_apply(panel, diag_blocks, super_blocks, edge_supers)
        outgoing = jnp.where(send_live, panel[send_index], jnp.zeros((), jnp.bfloat16))
        incoming = lax.all_to_all(outgoing, "curve", split_axis=0, concat_axis=0, tiled=True)
        forward = jnp.einsum(
            "fcp,fqp->fcq", incoming, far_blocks, preferred_element_type=jnp.float32
        )
        result = result.at[recv_index].add(jnp.where(recv_live, forward, 0.0))
        mirror = jnp.einsum(
            "fcp,fpq->fcq", panel[recv_index], far_blocks, preferred_element_type=jnp.float32
        )
        mirror = jnp.where(recv_live, mirror, 0.0)
        returned = lax.all_to_all(mirror, "curve", split_axis=0, concat_axis=0, tiled=True)
        result = result.at[send_index].add(jnp.where(send_live, returned, 0.0))
        return result

    unit_panel = jnp.ones((rows_dev, 1, block_size), jnp.bfloat16)
    inv_root = lax.rsqrt(apply_w(unit_panel))
    start_blocks = start_panel.reshape(width, rows_dev, block_size).transpose(1, 0, 2)
    start_gram = lax.psum(gram_of(start_blocks, start_blocks), "curve") / total_points
    current = left_apply(lower_inverse(start_gram), start_blocks)
    change = jnp.zeros_like(current)
    for step in range(ITERS):
        scaled = (inv_root * current).astype(jnp.bfloat16)
        image = inv_root * apply_w(scaled)
        rayleigh = lax.psum(gram_of(current, image), "curve") / total_points
        resid = image - left_apply(rayleigh.T, current)
        trial = current + step_size * resid + momentum * change
        cross = lax.psum(gram_of(trial, trial), "curve") / total_points
        fresh = left_apply(lower_inverse(cross), trial)
        change = fresh - current
        current = fresh
    basis = current.transpose(1, 0, 2).reshape(width, rows_dev * block_size)
    update = change.transpose(1, 0, 2).reshape(width, rows_dev * block_size)
    return (basis, update)


def solution(mesh):
    return jax.shard_map(
        shards,
        mesh=mesh,
        in_specs=(
            P("curve", None, None),
            P("curve", None, None, None),
            P("curve", None, None),
            P("curve"),
            P("curve"),
            P(None, "curve"),
        ),
        out_specs=(P(None, "curve"), P(None, "curve")),
        check_vma=False,
    )
```

profile of v0, /device:TPU:1, one launch (start us, length us, event | category | flops | bytes accessed | tf_op | source)
XLA Modules:
  0.0 952.7 jit_solution(4395993751826965920)
XLA Ops:
  7.6 10.2 %all-to-all-start = ((bf16[128,2,128]{2,1,0:T(2,128)(2,1)}), bf16[128,2,128]{2,1,0:T(2,128)(2,1)S(1)}, u32[]{:S(2)}, u32[]{:S(2)}) async-start(bf16[128,2,128]{2,1,0:T(2,128)(2,1)} %bitcast.265), calls=%async_computation | async-start | bytes 131072 | tf_op jit(solution)/shard_map/all_to_all | solution.py:86
  17.8 10.4 %copy.58 = bf16[64,4,128,128]{3,2,0,1:T(8,128)(2,1)} copy(bf16[64,4,128,128]{3,2,1,0:T(8,128)(2,1)} %param.10) | data formatting | bytes 16777216 | tf_op args[1]
  36.0 66.3 %psum.35 = f32[64,64]{0,1:T(8,128)S(1)} all-reduce(f32[64,64]{0,1:T(8,128)S(1)} %fusion.51), channel_id=1, replica_groups=mesh['curve'=128] {'curve'}, use_global_device_ids=true, to_apply=%region_0.1 | all-reduce | flops 4096 | bytes 32768 | tf_op jit(solution)/shard_map/psum | solution.py:102
  144.3 7.8 fusion.66
  153.0 10.5 %constant_dynamic-update-slice_fusion = bf16[68,4,128,128]{3,2,0,1:T(8,128)(2,1)} fusion(bf16[68,4,128,128]{3,2,0,1:T(8,128)(2,1)} %constant_dynamic-update-slice_fusion.1, bf16[64,4,128,128]{3,2,1,0:T(8,128)(2,1)} %param.10), kind=kLoop, calls=%fused_computation.180 | loop fusion | bytes 16777216 | tf_op jit(solution)/shard_map/concatenate | solution.py:50
  196.9 11.0 %all-to-all-start.2 = ((bf16[256,64,128]{2,1,0:T(8,128)(2,1)}), bf16[256,64,128]{2,1,0:T(8,128)(2,1)}, u32[]{:S(2)}, u32[]{:S(2)}) async-start(bf16[256,64,128]{2,1,0:T(8,128)(2,1)} %broadcast_select_fusion.7), calls=%async_computation.2 | async-start | bytes 8388608 | tf_op jit(solution)/shard_map/all_to_all | solution.py:86
  207.9 10.3 %broadcast_select_fusion.4 = f32[256,64,128]{2,1,0:T(8,128)} fusion(pred[256]{0:T(512)(128)(4,1)S(1)} %broadcast_compare_fusion.1, bf16[256,64,128]{2,1,0:T(8,128)(2,1)} %gather_fusion.3, bf16[256,128,128]{2,1,0:T(8,128)(2,1)} %param.11), kind=kOutput, calls=%fused_computation.16 | convolution fusion | flops 538968064 | bytes 20971776 | tf_op jit(solution)/shard_map/fcp,fpq->fcq/dot_general | solution.py:91
  233.9 26.7 %all-to-all-done.2 = bf16[256,64,128]{2,1,0:T(8,128)(2,1)} async-done(((bf16[256,64,128]{2,1,0:T(8,128)(2,1)}), bf16[256,64,128]{2,1,0:T(8,128)(2,1)}, u32[]{:S(2)}, u32[]{:S(2)}) %all-to-all-start.2) | async-done | bytes 4194336 | tf_op jit(solution)/shard_map/all_to_all | solution.py:86
  260.6 6.3 all-to-all-start.3
  286.5 11.3 %broadcast_select_fusion.5 = f32[256,64,128]{2,1,0:T(8,128)} fusion(pred[256]{0:T(512)(128)(4,1)S(1)} %copy-done.18, bf16[256,64,128]{2,1,0:T(8,128)(2,1)} %all-to-all-done.2, bf16[256,128,128]{2,1,0:T(8,128)(2,1)S(1)} %bitcast.267), kind=kOutput, calls=%fused_computation.17 | convolution fusion | flops 538968064 | bytes 20971776 | tf_op jit(solution)/shard_map/fcp,fqp->fcq/dot_general | solution.py:87
  297.8 38.8 %scatter_fusion = f32[64,64,128]{2,1,0:T(8,128)} fusion(f32[64,64,128]{2,1,0:T(8,128)} %add_add_fusion.1, s32[256]{0:T(256)S(1)} %copy-done.31, f32[256,64,128]{2,1,0:T(8,128)} %broadcast_select_fusion.5), kind=kCustom, calls=%fused_computation.8 | custom fusion | flops 2097152 | bytes 25166848 | tf_op jit(solution)/shard_map/scatter-add | solution.py:90
  336.6 31.6 %all-to-all-done.3 = f32[256,64,128]{2,1,0:T(8,128)} async-done(((f32[256,64,128]{2,1,0:T(8,128)}), f32[256,64,128]{2,1,0:T(8,128)}, u32[]{:S(2)}, u32[]{:S(2)}) %all-to-all-start.3) | async-done | bytes 8388640 | tf_op jit(solution)/shard_map/all_to_all | solution.py:95
  374.3 39.0 %scatter_fusion.1 = f32[64,64,128]{2,1,0:T(8,128)} fusion(f32[64,64,128]{2,1,0:T(8,128)} %scatter_fusion, s32[256]{0:T(256)S(1)} %copy-done.28, f32[256,64,128]{2,1,0:T(8,128)} %broadcast_select_fusion.3), kind=kCustom, calls=%fused_computation.9 | custom fusion | flops 2097152 | bytes 25166848 | tf_op jit(solution)/shard_map/scatter-add | solution.py:96
  417.4 66.9 %psum.36 = f32[64,64]{0,1:T(8,128)S(1)} all-reduce(f32[64,64]{0,1:T(8,128)S(1)} %fusion.52), channel_id=1, replica_groups=mesh['curve'=128] {'curve'}, use_global_device_ids=true, to_apply=%region_7.10 | all-reduce | flops 4096 | bytes 32768 | tf_op jit(solution)/shard_map/psum | solution.py:108
  492.5 63.1 %psum.37 = f32[64,64]{0,1:T(8,128)S(1)} all-reduce(f32[64,64]{0,1:T(8,128)S(1)} %convolution_bitcast_fusion.3), channel_id=1, replica_groups=mesh['curve'=128] {'curve'}, use_global_device_ids=true, to_apply=%region_8.11 | all-reduce | flops 4096 | bytes 32768 | tf_op jit(solution)/shard_map/psum | solution.py:111
  587.5 11.4 %all-to-all-start.4 = ((bf16[256,64,128]{2,1,0:T(8,128)(2,1)}), bf16[256,64,128]{2,1,0:T(8,128)(2,1)}, u32[]{:S(2)}, u32[]{:S(2)}) async-start(bf16[256,64,128]{2,1,0:T(8,128)(2,1)} %broadcast_select_fusion.6), calls=%async_computation.4 | async-start | bytes 8388608 | tf_op jit(solution)/shard_map/all_to_all | solution.py:86
  598.8 10.3 %broadcast_select_fusion.1 = f32[256,64,128]{2,1,0:T(8,128)} fusion(pred[256]{0:T(512)(128)(4,1)S(1)} %copy-done.18, bf16[256,64,128]{2,1,0:T(8,128)(2,1)} %gather_fusion.5, bf16[256,128,128]{2,1,0:T(8,128)(2,1)} %param.11), kind=kOutput, calls=%fused_computation.13 | convolution fusion | flops 538968064 | bytes 20971776 | tf_op jit(solution)/shard_map/fcp,fpq->fcq/dot_general | solution.py:91
  624.8 26.8 %all-to-all-done.4 = bf16[256,64,128]{2,1,0:T(8,128)(2,1)} async-done(((bf16[256,64,128]{2,1,0:T(8,128)(2,1)}), bf16[256,64,128]{2,1,0:T(8,128)(2,1)}, u32[]{:S(2)}, u32[]{:S(2)}) %all-to-all-start.4) | async-done | bytes 4194336 | tf_op jit(solution)/shard_map/all_to_all | solution.py:86
  676.2 11.3 %broadcast_select_fusion.2 = f32[256,64,128]{2,1,0:T(8,128)} fusion(pred[256]{0:T(512)(128)(4,1)S(1)} %copy-done.19, bf16[256,64,128]{2,1,0:T(8,128)(2,1)} %all-to-all-done.4, bf16[256,128,128]{2,1,0:T(8,128)(2,1)S(1)} %bitcast.269), kind=kOutput, calls=%fused_computation.14 | convolution fusion | flops 538968064 | bytes 20971776 | tf_op jit(solution)/shard_map/fcp,fqp->fcq/dot_general | solution.py:87
  687.5 26.2 %scatter_fusion.2 = f32[64,64,128]{2,1,0:T(8,128)S(1)} fusion(f32[64,64,128]{2,1,0:T(8,128)S(1)} %add_add_fusion, s32[256]{0:T(256)S(1)} %copy-done.32, f32[256,64,128]{2,1,0:T(8,128)} %broadcast_select_fusion.2), kind=kCustom, calls=%fused_computation.10 | custom fusion | flops 2097152 | bytes 25166848 | tf_op jit(solution)/shard_map/scatter-add | solution.py:90
  713.7 45.4 %all-to-all-done.5 = f32[256,64,128]{2,1,0:T(8,128)} async-done(((f32[256,64,128]{2,1,0:T(8,128)}), f32[256,64,128]{2,1,0:T(8,128)}, u32[]{:S(2)}, u32[]{:S(2)}) %all-to-all-start.5) | async-done | bytes 8388640 | tf_op jit(solution)/shard_map/all_to_all | solution.py:95
  765.2 26.1 %scatter_fusion.3 = f32[64,64,128]{2,1,0:T(8,128)S(1)} fusion(f32[64,64,128]{2,1,0:T(8,128)S(1)} %scatter_fusion.2, s32[256]{0:T(256)S(1)} %copy-done.29, f32[256,64,128]{2,1,0:T(8,128)} %broadcast_select_fusion), kind=kCustom, calls=%fused_computation.11 | custom fusion | flops 2097152 | bytes 25166848 | tf_op jit(solution)/shard_map/scatter-add | solution.py:96
  794.9 66.9 %psum.38 = f32[64,64]{0,1:T(8,128)S(1)} all-reduce(f32[64,64]{0,1:T(8,128)S(1)} %fusion.57), channel_id=1, replica_groups=mesh['curve'=128] {'curve'}, use_global_device_ids=true, to_apply=%region_11.14 | all-reduce | flops 4096 | bytes 32768 | tf_op jit(solution)/shard_map/psum | solution.py:108
  870.3 63.1 %psum.39 = f32[64,64]{0,1:T(8,128)S(1)} all-reduce(f32[64,64]{0,1:T(8,128)S(1)} %convolution_bitcast_fusion.1), channel_id=1, replica_groups=mesh['curve'=128] {'curve'}, use_global_device_ids=true, to_apply=%region_12.15 | all-reduce | flops 4096 | bytes 32768 | tf_op jit(solution)/shard_map/psum | solution.py:111
  (236 shorter events, 253.5 us)
Async XLA Ops:
  0.6 30.5 %copy-start = (bf16[64,128,128]{2,1,0:T(8,128)(2,1)S(1)}, bf16[64,128,128]{2,1,0:T(8,128)(2,1)}, u32[]{:S(2)}) copy-start(bf16[64,128,128]{2,1,0:T(8,128)(2,1)} %param.9) | copy-start | bytes 6291460
  0.7 135.5 %collective-permute-start.1 = (bf16[4,1,128]{2,0,1:T(4,128)(2,1)S(1)}, bf16[4,1,128]{2,0,1:T(4,128)(2,1)S(1)}, u32[]{:S(2)}, u32[]{:S(2)}) collective-permute-start(bf16[4,1,128]{2,0,1:T(4,128)(2,1)S(1)} %broadcast.92), channel_id=1, source_target_pairs={{0,1},{1,2},{2,3},{3,4},{4,5},{5,6},{6,7},{7,8},{8,9},{9,10},{10,1... | collective-permute-start | bytes 3080 | tf_op jit(solution)/shard_map/ppermute | solution.py:19
  3.8 118.8 %collective-permute-start = (bf16[4,1,128]{2,0,1:T(4,128)(2,1)S(1)}, bf16[4,1,128]{2,0,1:T(4,128)(2,1)S(1)}, u32[]{:S(2)}, u32[]{:S(2)}) collective-permute-start(bf16[4,1,128]{2,0,1:T(4,128)(2,1)S(1)} %broadcast.92), channel_id=1, source_target_pairs={{1,0},{2,1},{3,2},{4,3},{5,4},{6,5},{7,6},{8,7},{9,8},{10,9},{11,1... | collective-permute-start | bytes 3080 | tf_op jit(solution)/shard_map/ppermute | solution.py:20
  4.4 188.4 %copy-start.24 = (pred[256]{0:T(512)(128)(4,1)}, pred[256]{0:T(512)(128)(4,1)S(1)}, u32[]{:S(2)}) copy-start(pred[256]{0:T(512)(128)(4,1)S(1)} %broadcast_compare_fusion) | copy-start | bytes 772
  5.1 169.7 %copy-start.27 = (s32[256]{0:T(256)}, s32[256]{0:T(256)S(1)}, u32[]{:S(2)}) copy-start(s32[256]{0:T(256)S(1)} %broadcast_maximum_fusion) | copy-start | bytes 3076
  5.8 166.9 %copy-start.30 = (s32[256]{0:T(256)}, s32[256]{0:T(256)S(1)}, u32[]{:S(2)}) copy-start(s32[256]{0:T(256)S(1)} %broadcast_maximum_fusion.1) | copy-start | bytes 3076
  5.8 108.6 %copy-start.38 = (s32[1024]{0:T(1024)}, s32[1024]{0:T(1024)S(1)}, u32[]{:S(2)}) copy-start(s32[1024]{0:T(1024)S(1)} %get-tuple-element.20) | copy-start | bytes 12292
  7.6 129.2 %all-to-all-start = ((bf16[128,2,128]{2,1,0:T(2,128)(2,1)}), bf16[128,2,128]{2,1,0:T(2,128)(2,1)S(1)}, u32[]{:S(2)}, u32[]{:S(2)}) async-start(bf16[128,2,128]{2,1,0:T(2,128)(2,1)} %bitcast.265), calls=%async_computation | async-start | bytes 131072 | tf_op jit(solution)/shard_map/all_to_all | solution.py:86
  29.3 122.8 %collective-permute-start.2 = (bf16[4,4,128,128]{3,2,0,1:T(8,128)(2,1)S(1)}, bf16[4,4,128,128]{3,2,0,1:T(8,128)(2,1)S(1)}, u32[]{:S(2)}, u32[]{:S(2)}) collective-permute-start(bf16[4,4,128,128]{3,2,0,1:T(8,128)(2,1)S(1)} %slice.207), channel_id=1, source_target_pairs={{127,0},{0,1},{1,2},{2,3},{3,4},{4,5},{5,6},{6,7},{7,8},{8,9},{9,1... | collective-permute-start | bytes 1572872 | tf_op jit(solution)/shard_map/ppermute | solution.py:28
  31.1 176.7 %copy-start.17 = (pred[256]{0:T(512)(128)(4,1)}, pred[256]{0:T(512)(128)(4,1)S(1)}, u32[]{:S(2)}) copy-start(pred[256]{0:T(512)(128)(4,1)S(1)} %broadcast_compare_fusion.1) | copy-start | bytes 772
  137.4 37.4 %all-to-all-start.1 = ((f32[256,1,128]{2,1,0:T(1,128)}), f32[256,1,128]{2,1,0:T(1,128)S(1)}, u32[]{:S(2)}, u32[]{:S(2)}) async-start(f32[256,1,128]{2,1,0:T(1,128)} %bitcast.58), calls=%async_computation.1 | async-start | bytes 262144 | tf_op jit(solution)/shard_map/all_to_all | solution.py:95
  190.9 76.0 %collective-permute-start.4 = (bf16[4,64,128]{2,1,0:T(8,128)(2,1)}, bf16[4,64,128]{2,1,0:T(8,128)(2,1)}, u32[]{:S(2)}, u32[]{:S(2)}) collective-permute-start(bf16[4,64,128]{2,1,0:T(8,128)(2,1)} %get-tuple-element.6), channel_id=1, source_target_pairs={{0,1},{1,2},{2,3},{3,4},{4,5},{5,6},{6,7},{7,8},{8,9},{9,10},{10,1... | collective-permute-start | bytes 196616 | tf_op jit(solution)/shard_map/ppermute | solution.py:19
  192.9 28.1 %collective-permute-start.3 = (bf16[4,64,128]{2,1,0:T(8,128)(2,1)S(1)}, bf16[4,64,128]{2,1,0:T(8,128)(2,1)S(1)}, u32[]{:S(2)}, u32[]{:S(2)}) collective-permute-start(bf16[4,64,128]{2,1,0:T(8,128)(2,1)S(1)} %get-tuple-element.7), channel_id=1, source_target_pairs={{1,0},{2,1},{3,2},{4,3},{5,4},{6,5},{7,6},{8,7},{9,8},{10,9},{11,1... | collective-permute-start | bytes 196616 | tf_op jit(solution)/shard_map/ppermute | solution.py:20
  196.9 63.7 %all-to-all-start.2 = ((bf16[256,64,128]{2,1,0:T(8,128)(2,1)}), bf16[256,64,128]{2,1,0:T(8,128)(2,1)}, u32[]{:S(2)}, u32[]{:S(2)}) async-start(bf16[256,64,128]{2,1,0:T(8,128)(2,1)} %broadcast_select_fusion.7), calls=%async_computation.2 | async-start | bytes 8388608 | tf_op jit(solution)/shard_map/all_to_all | solution.py:86
  260.6 107.6 %all-to-all-start.3 = ((f32[256,64,128]{2,1,0:T(8,128)}), f32[256,64,128]{2,1,0:T(8,128)}, u32[]{:S(2)}, u32[]{:S(2)}) async-start(f32[256,64,128]{2,1,0:T(8,128)} %broadcast_select_fusion.4), calls=%async_computation.3 | async-start | bytes 16777216 | tf_op jit(solution)/shard_map/all_to_all | solution.py:95
  297.8 70.5 %copy-start.25 = (pred[256]{0:T(512)(128)(4,1)S(1)}, pred[256]{0:T(512)(128)(4,1)}, u32[]{:S(2)}) copy-start(pred[256]{0:T(512)(128)(4,1)} %copy-done.24) | copy-start | bytes 772
  336.6 37.6 %copy-start.28 = (s32[256]{0:T(256)S(1)}, s32[256]{0:T(256)}, u32[]{:S(2)}) copy-start(s32[256]{0:T(256)} %copy-done.27) | copy-start | bytes 3076
  374.3 39.0 %copy-start.11 = (f32[64,128]{1,0:T(8,128)S(1)}, f32[64,128]{1,0:T(8,128)}, u32[]{:S(2)}) copy-start(f32[64,128]{1,0:T(8,128)} %copy-done.10) | copy-start | bytes 98308
  582.1 75.7 %collective-permute-start.6 = (bf16[4,64,128]{2,1,0:T(8,128)(2,1)}, bf16[4,64,128]{2,1,0:T(8,128)(2,1)}, u32[]{:S(2)}, u32[]{:S(2)}) collective-permute-start(bf16[4,64,128]{2,1,0:T(8,128)(2,1)} %get-tuple-element.4), channel_id=1, source_target_pairs={{0,1},{1,2},{2,3},{3,4},{4,5},{5,6},{6,7},{7,8},{8,9},{9,10},{10,1... | collective-permute-start | bytes 196616 | tf_op jit(solution)/shard_map/ppermute | solution.py:19
  583.3 28.6 %collective-permute-start.5 = (bf16[4,64,128]{2,1,0:T(8,128)(2,1)S(1)}, bf16[4,64,128]{2,1,0:T(8,128)(2,1)S(1)}, u32[]{:S(2)}, u32[]{:S(2)}) collective-permute-start(bf16[4,64,128]{2,1,0:T(8,128)(2,1)S(1)} %get-tuple-element.5), channel_id=1, source_target_pairs={{1,0},{2,1},{3,2},{4,3},{5,4},{6,5},{7,6},{8,7},{9,8},{10,9},{11,1... | collective-permute-start | bytes 196616 | tf_op jit(solution)/shard_map/ppermute | solution.py:20
  587.5 64.1 %all-to-all-start.4 = ((bf16[256,64,128]{2,1,0:T(8,128)(2,1)}), bf16[256,64,128]{2,1,0:T(8,128)(2,1)}, u32[]{:S(2)}, u32[]{:S(2)}) async-start(bf16[256,64,128]{2,1,0:T(8,128)(2,1)} %broadcast_select_fusion.6), calls=%async_computation.4 | async-start | bytes 8388608 | tf_op jit(solution)/shard_map/all_to_all | solution.py:86
  651.6 107.6 %all-to-all-start.5 = ((f32[256,64,128]{2,1,0:T(8,128)}), f32[256,64,128]{2,1,0:T(8,128)}, u32[]{:S(2)}, u32[]{:S(2)}) async-start(f32[256,64,128]{2,1,0:T(8,128)} %broadcast_select_fusion.1), calls=%async_computation.5 | async-start | bytes 16777216 | tf_op jit(solution)/shard_map/all_to_all | solution.py:95
  687.5 71.7 %copy-start.26 = (pred[256]{0:T(512)(128)(4,1)S(1)}, pred[256]{0:T(512)(128)(4,1)}, u32[]{:S(2)}) copy-start(pred[256]{0:T(512)(128)(4,1)} %copy-done.24) | copy-start | bytes 772
  713.7 51.5 %copy-start.29 = (s32[256]{0:T(256)S(1)}, s32[256]{0:T(256)}, u32[]{:S(2)}) copy-start(s32[256]{0:T(256)} %copy-done.27) | copy-start | bytes 3076
  (45 other events, 284.2 us)
where the time goes:
time: 962 us; the launch traced here: 953 us
  blocking collectives  326 us (34%)
  other arithmetic  195 us (20%)
  matrix products  189 us (20%)
  waiting for transfers between devices  131 us (14%)
  starting transfers between devices  59.2 us (6%)
  local copies, waits for them, and re-layouts  50.7 us (5%)
    psum x2, blocking collectives, shards(): rayleigh = lax.psum(gram_of(current, image), 'curve') / total_points  134 us
    psum x2, blocking collectives, shards(): cross = lax.psum(gram_of(trial, trial), 'curve') / total_points  126 us
    all_to_all x3, waiting for transfers between devices, apply_w(): lax.all_to_all(mirror, 'curve', split_axis=0, concat_axis=0, tiled=True)  77 us
    scatter-add x3, other arithmetic, apply_w(): result = result.at[send_index].add(jnp.where(send_live, returned, 0.0))  67.2 us
    scatter-add x3, other arithmetic, apply_w(): result = result.at[recv_index].add(jnp.where(recv_live, forward, 0.0))  67.1 us
    psum x1, blocking collectives, shards(): lax.psum(gram_of(start_blocks, start_blocks), 'curve') / total_points  66.3 us
    all_to_all x3, waiting for transfers between devices, apply_w(): lax.all_to_all(outgoing, 'curve', split_axis=0, concat_axis=0, tiled=True)  53.5 us
    dot_general x12, matrix products, near_apply(): jnp.einsum('bcp,bpq->bcq', behind, supers_ext[first:first + rows_dev, ban...  42.3 us
  transfers between devices with their start and end apart: 13, of which 4 were waited for; matrix products, arithmetic and copies ran while one was open for 28% of the time, Pallas kernels for 0%

commit v1 on v0

--- a/solution.py
+++ b/solution.py
@@ -105,7 +105,7 @@
     for step in range(ITERS):
         scaled = (inv_root * current).astype(jnp.bfloat16)
         image = inv_root * apply_w(scaled)
-        rayleigh = lax.psum(gram_of(current, image), "curve") / total_points
+        rayleigh = jnp.sum(lax.all_gather(gram_of(current, image), "curve"), axis=0) / total_points
         resid = image - left_apply(rayleigh.T, current)
         trial = current + step_size * resid + momentum * change
         cross = lax.psum(gram_of(trial, trial), "curve") / total_points

time: 962 us -> 987 us (1.026)
  waiting for transfers between devices: 131 us -> 268 us
  blocking collectives: 326 us -> 192 us
  between operations: 1.56 us -> 15.3 us
    all_gather x0 -> x2, waiting for transfers between devices: none -> 141 us  [shards(): lax.all_gather(gram_of(current, image), 'curve')]
    psum x2 -> x0, blocking collectives: 134 us -> none  [shards(): rayleigh = lax.psum(gram_of(current, image), 'curve') / total_points]
  transfers between devices with their start and end apart: 13 -> 15, of which waited for: 4 -> 6; matrix products, arithmetic and copies ran while one was open for 28% -> 27% of each run, Pallas kernels for 0% -> 0%
where the time goes in v1:
time: 987 us; the launch traced here: 978 us
  waiting for transfers between devices  268 us (27%)
  other arithmetic  202 us (20%)
  blocking collectives  192 us (19%)
  matrix products  191 us (19%)
  starting transfers between devices  58.8 us (6%)
  local copies, waits for them, and re-layouts  51 us (5%)
  between operations  15.3 us (2%)
    all_gather x2, waiting for transfers between devices, shards(): lax.all_gather(gram_of(current, image), 'curve')  141 us
    psum x2, blocking collectives, shards(): cross = lax.psum(gram_of(trial, trial), 'curve') / total_points  125 us
    all_to_all x3, waiting for transfers between devices, apply_w(): lax.all_to_all(mirror, 'curve', split_axis=0, concat_axis=0, tiled=True)  73.7 us
    scatter-add x3, other arithmetic, apply_w(): result = result.at[recv_index].add(jnp.where(recv_live, forward, 0.0))  68.8 us
    scatter-add x3, other arithmetic, apply_w(): result = result.at[send_index].add(jnp.where(send_live, returned, 0.0))  67.2 us
    psum x1, blocking collectives, shards(): lax.psum(gram_of(start_blocks, start_blocks), 'curve') / total_points  66.3 us
    all_to_all x3, waiting for transfers between devices, apply_w(): lax.all_to_all(outgoing, 'curve', split_axis=0, concat_axis=0, tiled=True)  53.2 us
    dot_general x12, matrix products, near_apply(): jnp.einsum('bcp,bpq->bcq', behind, supers_ext[first:first + rows_dev, ban...  42.3 us
  transfers between devices with their start and end apart: 15, of which 6 were waited for; matrix products, arithmetic and copies ran while one was open for 27% of the time, Pallas kernels for 0%

profile of v1, /device:TPU:1, one launch (start us, length us, event | category | flops | bytes accessed | tf_op | source)
XLA Modules:
  0.0 977.6 jit_solution(4233618599151227738)
XLA Ops:
  14.1 10.2 %all-to-all-start = ((bf16[128,2,128]{2,1,0:T(2,128)(2,1)}), bf16[128,2,128]{2,1,0:T(2,128)(2,1)S(1)}, u32[]{:S(2)}, u32[]{:S(2)}) async-start(bf16[128,2,128]{2,1,0:T(2,128)(2,1)} %bitcast.267), calls=%async_computation | async-start | bytes 131072 | tf_op jit(solution)/shard_map/all_to_all | solution.py:86
  24.3 10.4 %copy.58 = bf16[64,4,128,128]{3,2,0,1:T(8,128)(2,1)} copy(bf16[64,4,128,128]{3,2,1,0:T(8,128)(2,1)} %param.10) | data formatting | bytes 16777216 | tf_op args[1]
  42.5 66.3 %psum.21 = f32[64,64]{0,1:T(8,128)S(1)} all-reduce(f32[64,64]{0,1:T(8,128)S(1)} %fusion.51), channel_id=1, replica_groups=mesh['curve'=128] {'curve'}, use_global_device_ids=true, to_apply=%region_0.1 | all-reduce | flops 4096 | bytes 32768 | tf_op jit(solution)/shard_map/psum | solution.py:102
  150.8 7.8 fusion.66
  159.6 10.5 %constant_dynamic-update-slice_fusion = bf16[68,4,128,128]{3,2,0,1:T(8,128)(2,1)} fusion(bf16[68,4,128,128]{3,2,0,1:T(8,128)(2,1)} %constant_dynamic-update-slice_fusion.1, bf16[64,4,128,128]{3,2,1,0:T(8,128)(2,1)} %param.10), kind=kLoop, calls=%fused_computation.180 | loop fusion | bytes 16777216 | tf_op jit(solution)/shard_map/concatenate | solution.py:50
  203.5 11.0 %all-to-all-start.2 = ((bf16[256,64,128]{2,1,0:T(8,128)(2,1)}), bf16[256,64,128]{2,1,0:T(8,128)(2,1)}, u32[]{:S(2)}, u32[]{:S(2)}) async-start(bf16[256,64,128]{2,1,0:T(8,128)(2,1)} %broadcast_select_fusion.7), calls=%async_computation.2 | async-start | bytes 8388608 | tf_op jit(solution)/shard_map/all_to_all | solution.py:86
  214.5 10.3 %broadcast_select_fusion.4 = f32[256,64,128]{2,1,0:T(8,128)} fusion(pred[256]{0:T(512)(128)(4,1)S(1)} %broadcast_compare_fusion.1, bf16[256,64,128]{2,1,0:T(8,128)(2,1)} %gather_fusion.3, bf16[256,128,128]{2,1,0:T(8,128)(2,1)} %param.11), kind=kOutput, calls=%fused_computation.16 | convolution fusion | flops 538968064 | bytes 20971776 | tf_op jit(solution)/shard_map/fcp,fpq->fcq/dot_general | solution.py:91
  240.6 26.7 %all-to-all-done.2 = bf16[256,64,128]{2,1,0:T(8,128)(2,1)} async-done(((bf16[256,64,128]{2,1,0:T(8,128)(2,1)}), bf16[256,64,128]{2,1,0:T(8,128)(2,1)}, u32[]{:S(2)}, u32[]{:S(2)}) %all-to-all-start.2) | async-done | bytes 4194336 | tf_op jit(solution)/shard_map/all_to_all | solution.py:86
  286.7 6.1 add_add_fusion.1
  292.9 11.3 %broadcast_select_fusion.5 = f32[256,64,128]{2,1,0:T(8,128)} fusion(pred[256]{0:T(512)(128)(4,1)S(1)} %copy-done.18, bf16[256,64,128]{2,1,0:T(8,128)(2,1)} %all-to-all-done.2, bf16[256,128,128]{2,1,0:T(8,128)(2,1)S(1)} %bitcast.269), kind=kOutput, calls=%fused_computation.17 | convolution fusion | flops 538968064 | bytes 20971776 | tf_op jit(solution)/shard_map/fcp,fqp->fcq/dot_general | solution.py:87
  304.2 40.3 %scatter_fusion = f32[64,64,128]{2,1,0:T(8,128)} fusion(f32[64,64,128]{2,1,0:T(8,128)} %add_add_fusion.1, s32[256]{0:T(256)S(1)} %copy-done.31, f32[256,64,128]{2,1,0:T(8,128)} %broadcast_select_fusion.5), kind=kCustom, calls=%fused_computation.8 | custom fusion | flops 2097152 | bytes 25166848 | tf_op jit(solution)/shard_map/scatter-add | solution.py:90
  344.4 29.3 %all-to-all-done.3 = f32[256,64,128]{2,1,0:T(8,128)} async-done(((f32[256,64,128]{2,1,0:T(8,128)}), f32[256,64,128]{2,1,0:T(8,128)}, u32[]{:S(2)}, u32[]{:S(2)}) %all-to-all-start.3) | async-done | bytes 8388640 | tf_op jit(solution)/shard_map/all_to_all | solution.py:95
  379.9 39.0 %scatter_fusion.1 = f32[64,64,128]{2,1,0:T(8,128)} fusion(f32[64,64,128]{2,1,0:T(8,128)} %scatter_fusion, s32[256]{0:T(256)S(1)} %copy-done.28, f32[256,64,128]{2,1,0:T(8,128)} %broadcast_select_fusion.3), kind=kCustom, calls=%fused_computation.9 | custom fusion | flops 2097152 | bytes 25166848 | tf_op jit(solution)/shard_map/scatter-add | solution.py:96
  423.6 71.6 %all-gather.5.cloned.1.call-done = f32[8192,64]{1,0:T(8,128)} async-done(((f32[64,64]{1,0:T(8,128)}), f32[8192,64]{1,0:T(8,128)}) %all-gather.5.cloned.1.call-update) | async-done | bytes 2097168 | tf_op jit(solution)/shard_map/all_gather | solution.py:108
  506.0 62.7 %psum.22 = f32[64,64]{0,1:T(8,128)S(1)} all-reduce(f32[64,64]{0,1:T(8,128)S(1)} %convolution_bitcast_fusion.3), channel_id=1, replica_groups=mesh['curve'=128] {'curve'}, use_global_device_ids=true, to_apply=%region_8.11 | all-reduce | flops 4096 | bytes 32768 | tf_op jit(solution)/shard_map/psum | solution.py:111
  601.2 11.1 %all-to-all-start.4 = ((bf16[256,64,128]{2,1,0:T(8,128)(2,1)}), bf16[256,64,128]{2,1,0:T(8,128)(2,1)}, u32[]{:S(2)}, u32[]{:S(2)}) async-start(bf16[256,64,128]{2,1,0:T(8,128)(2,1)} %broadcast_select_fusion.6), calls=%async_computation.4 | async-start | bytes 8388608 | tf_op jit(solution)/shard_map/all_to_all | solution.py:86
  612.3 10.3 %broadcast_select_fusion.1 = f32[256,64,128]{2,1,0:T(8,128)} fusion(pred[256]{0:T(512)(128)(4,1)S(1)} %copy-done.18, bf16[256,64,128]{2,1,0:T(8,128)(2,1)} %gather_fusion.5, bf16[256,128,128]{2,1,0:T(8,128)(2,1)} %param.11), kind=kOutput, calls=%fused_computation.13 | convolution fusion | flops 538968064 | bytes 20971776 | tf_op jit(solution)/shard_map/fcp,fpq->fcq/dot_general | solution.py:91
  638.3 26.5 %all-to-all-done.4 = bf16[256,64,128]{2,1,0:T(8,128)(2,1)} async-done(((bf16[256,64,128]{2,1,0:T(8,128)(2,1)}), bf16[256,64,128]{2,1,0:T(8,128)(2,1)}, u32[]{:S(2)}, u32[]{:S(2)}) %all-to-all-start.4) | async-done | bytes 4194336 | tf_op jit(solution)/shard_map/all_to_all | solution.py:86
  689.2 11.3 %broadcast_select_fusion.2 = f32[256,64,128]{2,1,0:T(8,128)} fusion(pred[256]{0:T(512)(128)(4,1)S(1)} %copy-done.19, bf16[256,64,128]{2,1,0:T(8,128)(2,1)} %all-to-all-done.4, bf16[256,128,128]{2,1,0:T(8,128)(2,1)S(1)} %bitcast.271), kind=kOutput, calls=%fused_computation.14 | convolution fusion | flops 538968064 | bytes 20971776 | tf_op jit(solution)/shard_map/fcp,fqp->fcq/dot_general | solution.py:87
  700.6 26.5 %scatter_fusion.2 = f32[64,64,128]{2,1,0:T(8,128)S(1)} fusion(f32[64,64,128]{2,1,0:T(8,128)S(1)} %add_add_fusion, s32[256]{0:T(256)S(1)} %copy-done.32, f32[256,64,128]{2,1,0:T(8,128)} %broadcast_select_fusion.2), kind=kCustom, calls=%fused_computation.10 | custom fusion | flops 2097152 | bytes 25166848 | tf_op jit(solution)/shard_map/scatter-add | solution.py:90
  727.1 44.3 %all-to-all-done.5 = f32[256,64,128]{2,1,0:T(8,128)} async-done(((f32[256,64,128]{2,1,0:T(8,128)}), f32[256,64,128]{2,1,0:T(8,128)}, u32[]{:S(2)}, u32[]{:S(2)}) %all-to-all-start.5) | async-done | bytes 8388640 | tf_op jit(solution)/shard_map/all_to_all | solution.py:95
  777.4 26.1 %scatter_fusion.3 = f32[64,64,128]{2,1,0:T(8,128)S(1)} fusion(f32[64,64,128]{2,1,0:T(8,128)S(1)} %scatter_fusion.2, s32[256]{0:T(256)S(1)} %copy-done.29, f32[256,64,128]{2,1,0:T(8,128)} %broadcast_select_fusion), kind=kCustom, calls=%fused_computation.11 | custom fusion | flops 2097152 | bytes 25166848 | tf_op jit(solution)/shard_map/scatter-add | solution.py:96
  807.7 69.4 %all-gather.7.cloned.1.call-done = f32[8192,64]{1,0:T(8,128)} async-done(((f32[64,64]{1,0:T(8,128)}), f32[8192,64]{1,0:T(8,128)}) %all-gather.7.cloned.1.call-update) | async-done | bytes 2097168 | tf_op jit(solution)/shard_map/all_gather | solution.py:108
  888.3 62.8 %psum.23 = f32[64,64]{0,1:T(8,128)S(1)} all-reduce(f32[64,64]{0,1:T(8,128)S(1)} %convolution_bitcast_fusion.1), channel_id=1, replica_groups=mesh['curve'=128] {'curve'}, use_global_device_ids=true, to_apply=%region_12.15 | all-reduce | flops 4096 | bytes 32768 | tf_op jit(solution)/shard_map/psum | solution.py:111
  (244 shorter events, 260.3 us)
Async XLA Ops:
  7.2 135.5 %collective-permute-start.1 = (bf16[4,1,128]{2,0,1:T(4,128)(2,1)S(1)}, bf16[4,1,128]{2,0,1:T(4,128)(2,1)S(1)}, u32[]{:S(2)}, u32[]{:S(2)}) collective-permute-start(bf16[4,1,128]{2,0,1:T(4,128)(2,1)S(1)} %broadcast.92), channel_id=1, source_target_pairs={{0,1},{1,2},{2,3},{3,4},{4,5},{5,6},{6,7},{7,8},{8,9},{9,10},{10,1... | collective-permute-start | bytes 3080 | tf_op jit(solution)/shard_map/ppermute | solution.py:19
  10.3 118.8 %collective-permute-start = (bf16[4,1,128]{2,0,1:T(4,128)(2,1)S(1)}, bf16[4,1,128]{2,0,1:T(4,128)(2,1)S(1)}, u32[]{:S(2)}, u32[]{:S(2)}) collective-permute-start(bf16[4,1,128]{2,0,1:T(4,128)(2,1)S(1)} %broadcast.92), channel_id=1, source_target_pairs={{1,0},{2,1},{3,2},{4,3},{5,4},{6,5},{7,6},{8,7},{9,8},{10,9},{11,1... | collective-permute-start | bytes 3080 | tf_op jit(solution)/shard_map/ppermute | solution.py:20
  11.0 188.6 %copy-start.24 = (pred[256]{0:T(512)(128)(4,1)}, pred[256]{0:T(512)(128)(4,1)S(1)}, u32[]{:S(2)}) copy-start(pred[256]{0:T(512)(128)(4,1)S(1)} %broadcast_compare_fusion) | copy-start | bytes 772
  11.7 169.7 %copy-start.27 = (s32[256]{0:T(256)}, s32[256]{0:T(256)S(1)}, u32[]{:S(2)}) copy-start(s32[256]{0:T(256)S(1)} %broadcast_maximum_fusion) | copy-start | bytes 3076
  12.3 166.9 %copy-start.30 = (s32[256]{0:T(256)}, s32[256]{0:T(256)S(1)}, u32[]{:S(2)}) copy-start(s32[256]{0:T(256)S(1)} %broadcast_maximum_fusion.1) | copy-start | bytes 3076
  12.4 108.6 %copy-start.38 = (s32[1024]{0:T(1024)}, s32[1024]{0:T(1024)S(1)}, u32[]{:S(2)}) copy-start(s32[1024]{0:T(1024)S(1)} %get-tuple-element.20) | copy-start | bytes 12292
  14.1 129.2 %all-to-all-start = ((bf16[128,2,128]{2,1,0:T(2,128)(2,1)}), bf16[128,2,128]{2,1,0:T(2,128)(2,1)S(1)}, u32[]{:S(2)}, u32[]{:S(2)}) async-start(bf16[128,2,128]{2,1,0:T(2,128)(2,1)} %bitcast.267), calls=%async_computation | async-start | bytes 131072 | tf_op jit(solution)/shard_map/all_to_all | solution.py:86
  35.8 122.8 %collective-permute-start.2 = (bf16[4,4,128,128]{3,2,0,1:T(8,128)(2,1)S(1)}, bf16[4,4,128,128]{3,2,0,1:T(8,128)(2,1)S(1)}, u32[]{:S(2)}, u32[]{:S(2)}) collective-permute-start(bf16[4,4,128,128]{3,2,0,1:T(8,128)(2,1)S(1)} %slice.207), channel_id=1, source_target_pairs={{127,0},{0,1},{1,2},{2,3},{3,4},{4,5},{5,6},{6,7},{7,8},{8,9},{9,1... | collective-permute-start | bytes 1572872 | tf_op jit(solution)/shard_map/ppermute | solution.py:28
  37.7 176.8 %copy-start.17 = (pred[256]{0:T(512)(128)(4,1)}, pred[256]{0:T(512)(128)(4,1)S(1)}, u32[]{:S(2)}) copy-start(pred[256]{0:T(512)(128)(4,1)S(1)} %broadcast_compare_fusion.1) | copy-start | bytes 772
  144.0 37.4 %all-to-all-start.1 = ((f32[256,1,128]{2,1,0:T(1,128)}), f32[256,1,128]{2,1,0:T(1,128)S(1)}, u32[]{:S(2)}, u32[]{:S(2)}) async-start(f32[256,1,128]{2,1,0:T(1,128)} %bitcast.58), calls=%async_computation.1 | async-start | bytes 262144 | tf_op jit(solution)/shard_map/all_to_all | solution.py:95
  197.5 75.7 %collective-permute-start.4 = (bf16[4,64,128]{2,1,0:T(8,128)(2,1)}, bf16[4,64,128]{2,1,0:T(8,128)(2,1)}, u32[]{:S(2)}, u32[]{:S(2)}) collective-permute-start(bf16[4,64,128]{2,1,0:T(8,128)(2,1)} %get-tuple-element.6), channel_id=1, source_target_pairs={{0,1},{1,2},{2,3},{3,4},{4,5},{5,6},{6,7},{7,8},{8,9},{9,10},{10,1... | collective-permute-start | bytes 196616 | tf_op jit(solution)/shard_map/ppermute | solution.py:19
  199.5 28.2 %collective-permute-start.3 = (bf16[4,64,128]{2,1,0:T(8,128)(2,1)S(1)}, bf16[4,64,128]{2,1,0:T(8,128)(2,1)S(1)}, u32[]{:S(2)}, u32[]{:S(2)}) collective-permute-start(bf16[4,64,128]{2,1,0:T(8,128)(2,1)S(1)} %get-tuple-element.7), channel_id=1, source_target_pairs={{1,0},{2,1},{3,2},{4,3},{5,4},{6,5},{7,6},{8,7},{9,8},{10,9},{11,1... | collective-permute-start | bytes 196616 | tf_op jit(solution)/shard_map/ppermute | solution.py:20
  203.5 63.7 %all-to-all-start.2 = ((bf16[256,64,128]{2,1,0:T(8,128)(2,1)}), bf16[256,64,128]{2,1,0:T(8,128)(2,1)}, u32[]{:S(2)}, u32[]{:S(2)}) async-start(bf16[256,64,128]{2,1,0:T(8,128)(2,1)} %broadcast_select_fusion.7), calls=%async_computation.2 | async-start | bytes 8388608 | tf_op jit(solution)/shard_map/all_to_all | solution.py:86
  267.3 106.5 %all-to-all-start.3 = ((f32[256,64,128]{2,1,0:T(8,128)}), f32[256,64,128]{2,1,0:T(8,128)}, u32[]{:S(2)}, u32[]{:S(2)}) async-start(f32[256,64,128]{2,1,0:T(8,128)} %broadcast_select_fusion.4), calls=%async_computation.3 | async-start | bytes 16777216 | tf_op jit(solution)/shard_map/all_to_all | solution.py:95
  272.9 222.2 %all-gather.5.cloned.1.call-start = ((), (), s32[]{:S(2)}) async-start(), calls=%async_computation.6 | async-start | bytes 4227072 | tf_op jit(solution)/shard_map/all_gather | solution.py:108
  304.2 69.6 %copy-start.25 = (pred[256]{0:T(512)(128)(4,1)S(1)}, pred[256]{0:T(512)(128)(4,1)}, u32[]{:S(2)}) copy-start(pred[256]{0:T(512)(128)(4,1)} %copy-done.24) | copy-start | bytes 772
  379.9 39.0 %copy-start.11 = (f32[64,128]{1,0:T(8,128)S(1)}, f32[64,128]{1,0:T(8,128)}, u32[]{:S(2)}) copy-start(f32[64,128]{1,0:T(8,128)} %copy-done.10) | copy-start | bytes 98308
  595.4 75.5 %collective-permute-start.6 = (bf16[4,64,128]{2,1,0:T(8,128)(2,1)}, bf16[4,64,128]{2,1,0:T(8,128)(2,1)}, u32[]{:S(2)}, u32[]{:S(2)}) collective-permute-start(bf16[4,64,128]{2,1,0:T(8,128)(2,1)} %get-tuple-element.4), channel_id=1, source_target_pairs={{0,1},{1,2},{2,3},{3,4},{4,5},{5,6},{6,7},{7,8},{8,9},{9,10},{10,1... | collective-permute-start | bytes 196616 | tf_op jit(solution)/shard_map/ppermute | solution.py:19
  597.1 28.4 %collective-permute-start.5 = (bf16[4,64,128]{2,1,0:T(8,128)(2,1)S(1)}, bf16[4,64,128]{2,1,0:T(8,128)(2,1)S(1)}, u32[]{:S(2)}, u32[]{:S(2)}) collective-permute-start(bf16[4,64,128]{2,1,0:T(8,128)(2,1)S(1)} %get-tuple-element.5), channel_id=1, source_target_pairs={{1,0},{2,1},{3,2},{4,3},{5,4},{6,5},{7,6},{8,7},{9,8},{10,9},{11,1... | collective-permute-start | bytes 196616 | tf_op jit(solution)/shard_map/ppermute | solution.py:20
  601.2 63.7 %all-to-all-start.4 = ((bf16[256,64,128]{2,1,0:T(8,128)(2,1)}), bf16[256,64,128]{2,1,0:T(8,128)(2,1)}, u32[]{:S(2)}, u32[]{:S(2)}) async-start(bf16[256,64,128]{2,1,0:T(8,128)(2,1)} %broadcast_select_fusion.6), calls=%async_computation.4 | async-start | bytes 8388608 | tf_op jit(solution)/shard_map/all_to_all | solution.py:86
  664.9 106.5 %all-to-all-start.5 = ((f32[256,64,128]{2,1,0:T(8,128)}), f32[256,64,128]{2,1,0:T(8,128)}, u32[]{:S(2)}, u32[]{:S(2)}) async-start(f32[256,64,128]{2,1,0:T(8,128)} %broadcast_select_fusion.1), calls=%async_computation.5 | async-start | bytes 16777216 | tf_op jit(solution)/shard_map/all_to_all | solution.py:95
  670.6 206.6 %all-gather.7.cloned.1.call-start = ((), (), s32[]{:S(2)}) async-start(), calls=%async_computation.7 | async-start | bytes 4227072 | tf_op jit(solution)/shard_map/all_gather | solution.py:108
  700.5 70.9 %copy-start.26 = (pred[256]{0:T(512)(128)(4,1)S(1)}, pred[256]{0:T(512)(128)(4,1)}, u32[]{:S(2)}) copy-start(pred[256]{0:T(512)(128)(4,1)} %copy-done.24) | copy-start | bytes 772
  727.1 50.4 %copy-start.29 = (s32[256]{0:T(256)S(1)}, s32[256]{0:T(256)}, u32[]{:S(2)}) copy-start(s32[256]{0:T(256)} %copy-done.27) | copy-start | bytes 3076
  (47 other events, 350.2 us)
Sparse Core Ops, SparseCore 0:
  423.7 71.4 all-gather.4
  807.8 69.2 all-gather.6
